TPU v7x, 512 devices: a whole 4x8x8 slice. The times are simulated.
512 devices in a mesh: grp: 16 (over z, core), sub: 32 (over y, x).
Axes of the slice: x: 4, y: 8, z: 8, core: 2. Of those that a mesh axis runs over, the one named last changes fastest.
Arguments:
- right_side: float32 [8192, 512], P(('grp', 'sub')), may hold values from -8 to 8
- metric: float32 [8192, 1536], P(('grp', 'sub')), may hold values from 0.3 to 3
- helmholtz: float32 [8192, 512], P(('grp', 'sub')), may hold values from 0.5 to 2
- jacobi: float32 [8192, 512], P(('grp', 'sub')), may hold values from 0.05 to 0.5
- pair_list: int32 [2, 524288], P(None, ('grp', 'sub')), may hold values from 0 to 8191
- shared_slots: int32 [512, 32, 128], P(('grp', 'sub')), may hold values from 0 to 8192, as said below
- face_points: int32 [2, 262144], P(None, ('grp', 'sub')), may hold values from 0 to 8191
- coarse_map: int32 [8, 8192], P(None, ('grp', 'sub')), may hold values from 0 to 63
- coarse_inverse: float32 [16, 64, 64], P('grp'), as said below
Outputs:
- solution: float32 [8192, 512], P(('grp', 'sub'))
- residual: float32 [8192, 512], P(('grp', 'sub'))
Inputs may be any that keep to these rules, and one draw needn't show every extreme that they name: `shared_slots`: entries equal to 8192 mark empty slots; the slot of device a for peer b in one group is filled exactly when the slot of b for a at the same position is; a device's slots for itself are empty; filled slots come first in each row. `coarse_inverse`: each group's matrix is symmetric and positive definite.
All inputs are finite; a program needn't handle non-finite values.
Results may differ from a plain program's by a relative error of at most 0.0003.
Values sent between devices are 32-bit elements; how exact they have to be, the bound alone decides.
A program may use at most 64 MiB of HBM per device.

v0:
```python
import jax
import jax.numpy as jnp
import numpy as np
from jax import lax
from jax.sharding import PartitionSpec as P

ITERS = 2
NC = 64


def extended(cells, sides, width):
    for axis, dim in sides:
        count = lax.axis_size(axis)
        ends = count - 1
        head = lax.slice_in_dim(cells, 0, width, axis=dim)
        tail = lax.slice_in_dim(cells, cells.shape[dim] - width, cells.shape[dim], axis=dim)
        cells = jnp.concatenate(
            [
                lax.ppermute(tail, axis, [(i, (i + 1) % count) for i in range(ends)]),
                cells,
                lax.ppermute(head, axis, [((i + 1) % count, i) for i in range(ends)]),
            ],
            axis=dim,
        )
    return cells


def tables():
    order_index = np.arange(8)
    colloc = np.cos(np.pi * order_index / 7.0)
    end_weights = (
        np.where((order_index == 0) | (order_index == 7), 2.0, 1.0) * (-1.0) ** order_index
    )
    spacing = colloc[:, None] - colloc[None, :] + np.eye(8)
    raw_matrix = np.outer(end_weights, 1.0 / end_weights) / spacing
    off_part = raw_matrix * (1.0 - np.eye(8))
    derivative = 0.25 * (off_part - np.eye(8) * off_part.sum(axis=1)[:, None])
    along_first = np.kron(derivative, np.eye(64)).T
    along_inner = np.concatenate(
        [np.kron(derivative, np.eye(8)).T, np.kron(np.eye(8), derivative).T], axis=1
    )
    point_index = np.arange(512)
    corner_index = np.arange(8)
    sign_first = 1.0 - 2.0 * (corner_index >> 2 & 1)
    sign_second = 1.0 - 2.0 * (corner_index >> 1 & 1)
    sign_third = 1.0 - 2.0 * (corner_index & 1)
    node_first = colloc[point_index // 64][:, None]
    node_second = colloc[point_index // 8 % 8][:, None]
    node_third = colloc[point_index % 8][:, None]
    corner = (
        0.5
        * (1.0 + sign_first[None, :] * node_first)
        * (0.5 * (1.0 + sign_second[None, :] * node_second))
        * (0.5 * (1.0 + sign_third[None, :] * node_third))
    )
    return (
        jnp.asarray(along_first, jnp.float32),
        jnp.asarray(along_inner, jnp.float32),
        jnp.asarray(corner, jnp.float32),
    )


def residual_product(resid, smoothed):
    return lax.psum(jnp.sum(resid * smoothed), ("grp", "sub"))


def body(
    right_side,
    metric,
    helmholtz,
    jacobi,
    pair_list,
    shared_slots,
    face_points,
    coarse_map,
    coarse_inverse,
):
    highest = lax.Precision.HIGHEST
    along_first, along_inner, corner = tables()
    elements = right_side.shape[0]
    points = elements * right_side.shape[1]
    slots = shared_slots[0]

    def assemble(field):
        flat = field.reshape(-1)
        total = (
            flat.at[pair_list[0]].add(flat[pair_list[1]]).at[pair_list[1]].add(flat[pair_list[0]])
        )
        padded = jnp.concatenate([flat, jnp.zeros((1,), jnp.float32)])
        sent = padded[slots]
        received = lax.all_to_all(sent, "sub", split_axis=0, concat_axis=0, tiled=True)
        total = (
            jnp.concatenate([total, jnp.zeros((1,), jnp.float32)]).at[slots].add(received)[:points]
        )
        face_values = flat[face_points]
        rim = extended(face_values, (("grp", 0),), 1)
        total = total.at[face_points[0]].add(rim[0]).at[face_points[1]].add(rim[3])
        return total.reshape(field.shape)

    onehot = (coarse_map.reshape(-1)[:, None] == jnp.arange(NC, dtype=jnp.int32)[None, :]).astype(
        jnp.float32
    )

    def precondition(resid):
        vertex = jnp.dot(resid, corner, precision=highest)
        partial_coarse = jnp.dot(vertex.T.reshape(-1), onehot, precision=highest)
        coarse = lax.psum(partial_coarse, "sub")
        solved = jnp.dot(coarse_inverse[0], coarse, precision=highest)
        at_vertex = jnp.dot(onehot, solved, precision=highest).reshape(8, -1)
        return jacobi * resid + jnp.dot(at_vertex.T, corner.T, precision=highest)

    solution = jnp.zeros_like(right_side)
    residual = right_side
    smoothed = precondition(residual)
    direction = smoothed
    rz_now = residual_product(residual, smoothed)
    for iteration in range(ITERS):
        summed = assemble(direction)
        grad_first = jnp.dot(summed, along_first, precision=highest)
        inner = jnp.dot(summed.reshape(elements * 8, 64), along_inner, precision=highest)
        grad_second = inner[:, :64].reshape(elements, 512)
        grad_third = inner[:, 64:].reshape(elements, 512)
        flux_first = metric[:, :512] * grad_first
        flux_second = (metric[:, 512:1024] * grad_second).reshape(elements * 8, 64)
        flux_third = (metric[:, 1024:] * grad_third).reshape(elements * 8, 64)
        back = jnp.dot(flux_first, along_first.T, precision=highest)
        fluxes = jnp.concatenate([flux_second, flux_third], axis=1)
        back = back + jnp.dot(fluxes, along_inner.T, precision=highest).reshape(elements, 512)
        image = assemble(back) + helmholtz * direction
        alpha = rz_now / lax.psum(jnp.sum(direction * image), ("grp", "sub"))
        solution = solution + alpha * direction
        residual = residual - alpha * image
        if iteration + 1 < ITERS:
            smoothed = precondition(residual)
            rz_new = residual_product(residual, smoothed)
            direction = smoothed + rz_new / rz_now * direction
            rz_now = rz_new
    return (solution, residual)


def solution(mesh):
    in_specs = (
        P(("grp", "sub"), None),
        P(("grp", "sub"), None),
        P(("grp", "sub"), None),
        P(("grp", "sub"), None),
        P(None, ("grp", "sub")),
        P(("grp", "sub"), None, None),
        P(None, ("grp", "sub")),
        P(None, ("grp", "sub")),
        P("grp", None, None),
    )
    out_specs = (P(("grp", "sub"), None), P(("grp", "sub"), None))
    return jax.shard_map(body, mesh=mesh, in_specs=in_specs, out_specs=out_specs, check_vma=False)
```

profile of v0, /device:TPU:1, one launch (start us, length us, event | category | flops | bytes accessed | tf_op | source)
XLA Modules:
  0.0 937.5 jit_solution(3076881587278794797)
XLA Ops:
  3.3 61.9 %psum.42 = f32[64]{0:T(128)S(1)} all-reduce(f32[64]{0:T(128)S(1)} %convolution_bitcast_fusion.5), channel_id=1, replica_groups=mesh['grp'=16,'sub'=32] {'sub'}, use_global_device_ids=true, to_apply=%region_0.0 | all-reduce | flops 64 | bytes 512 | tf_op jit(solution)/shard_map/psum | solution.py:107
  67.3 40.6 %gather_fusion.2 = f32[4096]{0:T(1024)} fusion(f32[8193]{0:T(1024)S(1)} %pad_maximum_fusion.6, s32[4096]{0:T(1024)S(1)} %broadcast_clamp_fusion), kind=kCustom, calls=%fused_computation.2 | custom fusion | bytes 49152 | tf_op jit(solution)/shard_map/gather | solution.py:90
  112.2 6.2 gather_fusion.3
  118.4 19.0 %collective-permute-start = (f32[1,512]{1,0:T(1,128)S(1)}, f32[1,512]{1,0:T(1,128)S(1)}, u32[]{:S(2)}, u32[]{:S(2)}) collective-permute-start(f32[1,512]{1,0:T(1,128)S(1)} %bitcast.169), channel_id=1, source_target_pairs={{0,32},{32,64},{64,96},{96,128},{128,160},{160,192},{192,224},{224... | collective-permute-start | bytes 6152 | tf_op jit(solution)/shard_map/ppermute | solution.py:19
  139.4 6.2 gather_fusion
  145.6 6.2 gather_fusion.1
  164.0 26.0 %scatter_fusion.2 = f32[8193]{0:T(1024)S(1)} fusion(f32[8193]{0:T(1024)S(1)} %pad_maximum_fusion.7, s32[4096]{0:T(1024)S(1)} %fusion.8, f32[4096]{0:T(1024)S(1)} %bitcast.146), kind=kCustom, calls=%fused_computation.18 | custom fusion | flops 4096 | bytes 65536 | tf_op jit(solution)/shard_map/scatter-add | solution.py:93
  201.8 6.2 gather_fusion.4
  207.9 6.2 gather_fusion.5
  214.1 6.2 gather_fusion.7
  220.3 40.6 %gather_fusion.6 = f32[4096]{0:T(1024)} fusion(f32[8193]{0:T(1024)S(1)} %pad_maximum_fusion.4, s32[4096]{0:T(1024)S(1)} %broadcast_clamp_fusion), kind=kCustom, calls=%fused_computation.6 | custom fusion | bytes 49152 | tf_op jit(solution)/shard_map/gather | solution.py:90
  273.0 9.4 %all-to-all-start.1 = ((f32[32,1,128]{2,1,0:T(1,128)}), f32[32,1,128]{2,1,0:T(1,128)S(1)}, u32[]{:S(2)}, u32[]{:S(2)}) async-start(f32[32,1,128]{2,1,0:T(1,128)} %bitcast.22), calls=%async_computation.1 | async-start | bytes 32768 | tf_op jit(solution)/shard_map/all_to_all | solution.py:91
  290.9 26.0 %scatter_fusion.7 = f32[8193]{0:T(1024)S(1)} fusion(f32[8193]{0:T(1024)S(1)} %pad_maximum_fusion.5, s32[4096]{0:T(1024)S(1)} %fusion.8, f32[4096]{0:T(1024)S(1)} %bitcast.148), kind=kCustom, calls=%fused_computation.23 | custom fusion | flops 4096 | bytes 65536 | tf_op jit(solution)/shard_map/scatter-add | solution.py:93
  325.1 101.2 %all-reduce = (f32[]{:T(128)}, f32[]{:T(128)}) all-reduce(f32[]{:T(128)} %get-tuple-element.3, f32[]{:T(128)} %get-tuple-element.2), channel_id=1, replica_groups=mesh['grp'=16,'sub'=32] {'grp','sub'}, use_global_device_ids=true, to_apply=%region_2.0 | all-reduce | flops 2 | bytes 16 | tf_op jit(solution)/shard_map/psum | solution.py:64
  428.5 56.9 %psum.45 = f32[64]{0:T(128)S(1)} all-reduce(f32[64]{0:T(128)S(1)} %convolution_bitcast_fusion.2), channel_id=1, replica_groups=mesh['grp'=16,'sub'=32] {'sub'}, use_global_device_ids=true, to_apply=%region_15.0 | all-reduce | flops 64 | bytes 512 | tf_op jit(solution)/shard_map/psum | solution.py:107
  486.9 107.3 %psum.46 = f32[]{:T(128)} all-reduce(f32[]{:T(128)} %get-tuple-element.28), channel_id=1, replica_groups=mesh['grp'=16,'sub'=32] {'grp','sub'}, use_global_device_ids=true, to_apply=%region_17.0 | all-reduce | flops 1 | bytes 8 | tf_op jit(solution)/shard_map/psum | solution.py:64
  595.7 6.2 gather_fusion.8
  614.2 40.6 %gather_fusion.10 = f32[4096]{0:T(1024)} fusion(f32[8193]{0:T(1024)S(1)} %pad_maximum_fusion.2, s32[4096]{0:T(1024)S(1)} %broadcast_clamp_fusion), kind=kCustom, calls=%fused_computation.10 | custom fusion | bytes 49152 | tf_op jit(solution)/shard_map/gather | solution.py:90
  666.9 7.2 all-to-all-start.2
  682.7 26.0 %scatter_fusion.12 = f32[8193]{0:T(1024)S(1)} fusion(f32[8193]{0:T(1024)S(1)} %pad_maximum_fusion.3, s32[4096]{0:T(1024)S(1)} %fusion.8, f32[4096]{0:T(1024)S(1)} %bitcast.149), kind=kCustom, calls=%fused_computation.28 | custom fusion | flops 4096 | bytes 65536 | tf_op jit(solution)/shard_map/scatter-add | solution.py:93
  737.4 40.6 %gather_fusion.14 = f32[4096]{0:T(1024)} fusion(f32[8193]{0:T(1024)S(1)} %pad_maximum_fusion, s32[4096]{0:T(1024)S(1)} %broadcast_clamp_fusion), kind=kCustom, calls=%fused_computation.14 | custom fusion | bytes 49152 | tf_op jit(solution)/shard_map/gather | solution.py:90
  790.2 7.6 all-to-all-start.3
  806.3 26.0 %scatter_fusion.17 = f32[8193]{0:T(1024)S(1)} fusion(f32[8193]{0:T(1024)S(1)} %pad_maximum_fusion.1, s32[4096]{0:T(1024)S(1)} %fusion.8, f32[4096]{0:T(1024)S(1)} %bitcast.147), kind=kCustom, calls=%fused_computation.33 | custom fusion | flops 4096 | bytes 65536 | tf_op jit(solution)/shard_map/scatter-add | solution.py:93
  839.7 95.6 %psum.47 = f32[]{:T(128)} all-reduce(f32[]{:T(128)} %multiply_reduce_fusion), channel_id=1, replica_groups=mesh['grp'=16,'sub'=32] {'grp','sub'}, use_global_device_ids=true, to_apply=%region_29.0 | all-reduce | flops 1 | bytes 8 | tf_op jit(solution)/shard_map/psum | solution.py:130
  (152 shorter events, 156.3 us)
Async XLA Ops:
  0.6 64.6 %copy-start = (f32[1,64,64]{2,1,0:T(8,128)S(1)}, f32[1,64,64]{2,1,0:T(8,128)}, u32[]{:S(2)}) copy-start(f32[1,64,64]{2,1,0:T(8,128)} %param.20) | copy-start | bytes 49156
  0.6 65.0 %copy-start.2 = (f32[512,8]{1,0:T(8,128)S(1)}, f32[512,8]{1,0:T(8,128)}, u32[]{:S(2)}) copy-start(f32[512,8]{1,0:T(8,128)} %constant.5.clone) | copy-start | bytes 49156
  65.3 0.8 copy-start.3
  65.3 0.8 copy-start.6
  107.8 4.3 copy-start.11
  107.8 56.2 %all-to-all-start = ((f32[32,1,128]{2,1,0:T(1,128)}), f32[32,1,128]{2,1,0:T(1,128)S(1)}, u32[]{:S(2)}, u32[]{:S(2)}) async-start(f32[32,1,128]{2,1,0:T(1,128)} %bitcast.12), calls=%async_computation | async-start | bytes 32768 | tf_op jit(solution)/shard_map/all_to_all | solution.py:91
  118.4 71.7 %collective-permute-start = (f32[1,512]{1,0:T(1,128)S(1)}, f32[1,512]{1,0:T(1,128)S(1)}, u32[]{:S(2)}, u32[]{:S(2)}) collective-permute-start(f32[1,512]{1,0:T(1,128)S(1)} %bitcast.169), channel_id=1, source_target_pairs={{0,32},{32,64},{64,96},{96,128},{128,160},{160,192},{192,224},{224... | collective-permute-start | bytes 6152 | tf_op jit(solution)/shard_map/ppermute | solution.py:19
  137.4 2.0 copy-start.12
  137.4 56.0 %collective-permute-start.1 = (f32[1,512]{1,0:T(1,128)S(1)}, f32[1,512]{1,0:T(1,128)S(1)}, u32[]{:S(2)}, u32[]{:S(2)}) collective-permute-start(f32[1,512]{1,0:T(1,128)S(1)} %bitcast.167), channel_id=1, source_target_pairs={{32,0},{64,32},{96,64},{128,96},{160,128},{192,160},{224,192},{256... | collective-permute-start | bytes 6152 | tf_op jit(solution)/shard_map/ppermute | solution.py:21
  193.4 4.0 copy-start.8
  193.5 4.6 copy-start.5
  197.3 2.8 copy-start.1
  198.2 0.8 copy-start.9
  199.0 0.8 copy-start.7
  273.0 17.9 %all-to-all-start.1 = ((f32[32,1,128]{2,1,0:T(1,128)}), f32[32,1,128]{2,1,0:T(1,128)S(1)}, u32[]{:S(2)}, u32[]{:S(2)}) async-start(f32[32,1,128]{2,1,0:T(1,128)} %bitcast.22), calls=%async_computation.1 | async-start | bytes 32768 | tf_op jit(solution)/shard_map/all_to_all | solution.py:91
  282.4 34.5 %collective-permute-start.2 = (f32[1,512]{1,0:T(1,128)S(1)}, f32[1,512]{1,0:T(1,128)S(1)}, u32[]{:S(2)}, u32[]{:S(2)}) collective-permute-start(f32[1,512]{1,0:T(1,128)S(1)} %bitcast.173), channel_id=1, source_target_pairs={{0,32},{32,64},{64,96},{96,128},{128,160},{160,192},{192,224},{224... | collective-permute-start | bytes 6152 | tf_op jit(solution)/shard_map/ppermute | solution.py:19
  286.3 34.0 %collective-permute-start.3 = (f32[1,512]{1,0:T(1,128)S(1)}, f32[1,512]{1,0:T(1,128)S(1)}, u32[]{:S(2)}, u32[]{:S(2)}) collective-permute-start(f32[1,512]{1,0:T(1,128)S(1)} %bitcast.170), channel_id=1, source_target_pairs={{32,0},{64,32},{96,64},{128,96},{160,128},{192,160},{224,192},{256... | collective-permute-start | bytes 6152 | tf_op jit(solution)/shard_map/ppermute | solution.py:21
  323.8 0.8 copy-start.4
  666.9 15.7 %all-to-all-start.2 = ((f32[32,1,128]{2,1,0:T(1,128)}), f32[32,1,128]{2,1,0:T(1,128)S(1)}, u32[]{:S(2)}, u32[]{:S(2)}) async-start(f32[32,1,128]{2,1,0:T(1,128)} %bitcast.33), calls=%async_computation.2 | async-start | bytes 32768 | tf_op jit(solution)/shard_map/all_to_all | solution.py:91
  674.1 34.5 %collective-permute-start.4 = (f32[1,512]{1,0:T(1,128)S(1)}, f32[1,512]{1,0:T(1,128)S(1)}, u32[]{:S(2)}, u32[]{:S(2)}) collective-permute-start(f32[1,512]{1,0:T(1,128)S(1)} %bitcast.174), channel_id=1, source_target_pairs={{0,32},{32,64},{64,96},{96,128},{128,160},{160,192},{192,224},{224... | collective-permute-start | bytes 6152 | tf_op jit(solution)/shard_map/ppermute | solution.py:19
  678.9 33.2 %collective-permute-start.5 = (f32[1,512]{1,0:T(1,128)S(1)}, f32[1,512]{1,0:T(1,128)S(1)}, u32[]{:S(2)}, u32[]{:S(2)}) collective-permute-start(f32[1,512]{1,0:T(1,128)S(1)} %bitcast.171), channel_id=1, source_target_pairs={{32,0},{64,32},{96,64},{128,96},{160,128},{192,160},{224,192},{256... | collective-permute-start | bytes 6152 | tf_op jit(solution)/shard_map/ppermute | solution.py:21
  790.2 16.1 %all-to-all-start.3 = ((f32[32,1,128]{2,1,0:T(1,128)}), f32[32,1,128]{2,1,0:T(1,128)S(1)}, u32[]{:S(2)}, u32[]{:S(2)}) async-start(f32[32,1,128]{2,1,0:T(1,128)} %bitcast.39), calls=%async_computation.3 | async-start | bytes 32768 | tf_op jit(solution)/shard_map/all_to_all | solution.py:91
  797.8 34.5 %collective-permute-start.6 = (f32[1,512]{1,0:T(1,128)S(1)}, f32[1,512]{1,0:T(1,128)S(1)}, u32[]{:S(2)}, u32[]{:S(2)}) collective-permute-start(f32[1,512]{1,0:T(1,128)S(1)} %bitcast.172), channel_id=1, source_target_pairs={{0,32},{32,64},{64,96},{96,128},{128,160},{160,192},{192,224},{224... | collective-permute-start | bytes 6152 | tf_op jit(solution)/shard_map/ppermute | solution.py:19
  801.6 34.1 %collective-permute-start.7 = (f32[1,512]{1,0:T(1,128)S(1)}, f32[1,512]{1,0:T(1,128)S(1)}, u32[]{:S(2)}, u32[]{:S(2)}) collective-permute-start(f32[1,512]{1,0:T(1,128)S(1)} %bitcast.168), channel_id=1, source_target_pairs={{32,0},{64,32},{96,64},{128,96},{160,128},{192,160},{224,192},{256... | collective-permute-start | bytes 6152 | tf_op jit(solution)/shard_map/ppermute | solution.py:21
  (1 other events, 0.7 us)
where the time goes:
time: 945 us; the launch traced here: 938 us
  blocking collectives  423 us (45%)
  local copies, waits for them, and re-layouts  242 us (26%)
  other arithmetic  183 us (19%)
  starting transfers between devices  67.7 us (7%)
    psum x2, blocking collectives, residual_product(): return lax.psum(jnp.sum(resid * smoothed), ('grp', 'sub'))  209 us
    gather x4, local copies, waits for them, and re-layouts, assemble(): sent = padded[slots]  162 us
    psum x2, blocking collectives, precondition(): coarse = lax.psum(partial_coarse, 'sub')  119 us
    scatter-add x4, other arithmetic, assemble(): jnp.concatenate([total, jnp.zeros((1,), jnp.float32)]).at[slots]  104 us
    psum x1, blocking collectives, body(): alpha = rz_now / lax.psum(jnp.sum(direction * image), ('grp', 'sub'))  95.6 us
    scatter-add x8, other arithmetic, assemble(): flat.at[pair_list[0]].add(flat[pair_list[1]]).at[pair_list[1]]  48.8 us
    ppermute x4, starting transfers between devices, extended(): lax.ppermute(tail, axis, [(i, (i + 1) % count) for i in range(ends)])  31.5 us
    all_to_all x4, starting transfers between devices, assemble(): lax.all_to_all(sent, 'sub', split_axis=0, concat_axis=0, tiled=True)  28.5 us
  transfers between devices with their start and end apart: 12, of which 3 were waited for; matrix products, arithmetic and copies ran while one was open for 16% of the time, Pallas kernels for 0%

commit v1 on v0

--- a/solution.py
+++ b/solution.py
@@ -104,7 +104,13 @@
     def precondition(resid):
         vertex = jnp.dot(resid, corner, precision=highest)
         partial_coarse = jnp.dot(vertex.T.reshape(-1), onehot, precision=highest)
-        coarse = lax.psum(partial_coarse, "sub")
+        size = lax.axis_size("sub")
+        coarse, reach = (partial_coarse, 1)
+        while reach < size:
+            coarse = coarse + lax.ppermute(
+                coarse, "sub", [(i_2, i_2 ^ reach) for i_2 in range(size)]
+            )
+            reach = 2 * reach
         solved = jnp.dot(coarse_inverse[0], coarse, precision=highest)
         at_vertex = jnp.dot(onehot, solved, precision=highest).reshape(8, -1)
         return jacobi * resid + jnp.dot(at_vertex.T, corner.T, precision=highest)

time: 945 us -> 871 us (0.922)
  blocking collectives: 423 us -> 297 us
  starting transfers between devices: 67.7 us -> 100 us
  waiting for transfers between devices: 7.23 us -> 25.4 us
    psum x2 -> x0, blocking collectives: 119 us -> none  [precondition(): coarse = lax.psum(partial_coarse, 'sub')]
    ppermute x0 -> x10, starting transfers between devices: none -> 38.7 us  [precondition(): lax.ppermute(coarse, 'sub', [(i_2, i_2 ^ reach) for i_2 in range(size)])]
    ppermute x0 -> x10, waiting for transfers between devices: none -> 16.5 us  [precondition(): lax.ppermute(coarse, 'sub', [(i_2, i_2 ^ reach) for i_2 in range(size)])]
    ppermute x4, starting transfers between devices: 31.5 us -> 21.5 us  [extended(): lax.ppermute(tail, axis, [(i, (i + 1) % count) for i in range(ends)])]
  transfers between devices with their start and end apart: 12 -> 22, of which waited for: 3 -> 12; matrix products, arithmetic and copies ran while one was open for 16% -> 14% of each run, Pallas kernels for 0% -> 0%
where the time goes in v1:
time: 871 us; the launch traced here: 863 us
  blocking collectives  297 us (34%)
  local copies, waits for them, and re-layouts  243 us (28%)
  other arithmetic  183 us (21%)
  starting transfers between devices  100 us (11%)
  waiting for transfers between devices  25.4 us (3%)
  matrix products  9.39 us (1%)
    psum x2, blocking collectives, residual_product(): return lax.psum(jnp.sum(resid * smoothed), ('grp', 'sub'))  200 us
    gather x4, local copies, waits for them, and re-layouts, assemble(): sent = padded[slots]  162 us
    scatter-add x4, other arithmetic, assemble(): jnp.concatenate([total, jnp.zeros((1,), jnp.float32)]).at[slots]  104 us
    psum x1, blocking collectives, body(): alpha = rz_now / lax.psum(jnp.sum(direction * image), ('grp', 'sub'))  97 us
    scatter-add x8, other arithmetic, assemble(): flat.at[pair_list[0]].add(flat[pair_list[1]]).at[pair_list[1]]  48.8 us
    ppermute x10, starting transfers between devices, precondition(): lax.ppermute(coarse, 'sub', [(i_2, i_2 ^ reach) for i_2 in range(size)])  38.7 us
    all_to_all x4, starting transfers between devices, assemble(): lax.all_to_all(sent, 'sub', split_axis=0, concat_axis=0, tiled=True)  32.3 us
    scatter-add x8, other arithmetic, assemble(): total = total.at[face_points[0]].add(rim[0]).at[face_points[1]].add(rim[3])  27.7 us
  transfers between devices with their start and end apart: 22, of which 12 were waited for; matrix products, arithmetic and copies ran while one was open for 14% of the time, Pallas kernels for 0%

profile of v1, /device:TPU:1, one launch (start us, length us, event | category | flops | bytes accessed | tf_op | source)
XLA Modules:
  0.0 863.1 jit_solution(16011451052271724641)
XLA Ops:
  23.9 7.4 collective-permute-start.4
  33.6 6.2 gather_fusion
  39.8 6.2 gather_fusion.1
  46.0 6.2 gather_fusion.3
  64.4 40.6 %gather_fusion.2 = f32[4096]{0:T(1024)} fusion(f32[8193]{0:T(1024)S(1)} %pad_maximum_fusion.6, s32[4096]{0:T(1024)S(1)} %broadcast_clamp_fusion), kind=kCustom, calls=%fused_computation.2 | custom fusion | bytes 49152 | tf_op jit(solution)/shard_map/gather | solution.py:90
  104.9 9.2 %all-to-all-start = ((f32[32,1,128]{2,1,0:T(1,128)}), f32[32,1,128]{2,1,0:T(1,128)S(1)}, u32[]{:S(2)}, u32[]{:S(2)}) async-start(f32[32,1,128]{2,1,0:T(1,128)} %bitcast.12), calls=%async_computation | async-start | bytes 32768 | tf_op jit(solution)/shard_map/all_to_all | solution.py:91
  114.2 10.6 %collective-permute-start.5 = (f32[1,512]{1,0:T(1,128)S(1)}, f32[1,512]{1,0:T(1,128)S(1)}, u32[]{:S(2)}, u32[]{:S(2)}) collective-permute-start(f32[1,512]{1,0:T(1,128)S(1)} %bitcast.172), channel_id=1, source_target_pairs={{0,32},{32,64},{64,96},{96,128},{128,160},{160,192},{192,224},{224... | collective-permute-start | bytes 6152 | tf_op jit(solution)/shard_map/ppermute | solution.py:19
  126.7 26.0 %scatter_fusion.2 = f32[8193]{0:T(1024)S(1)} fusion(f32[8193]{0:T(1024)S(1)} %pad_maximum_fusion.7, s32[4096]{0:T(1024)S(1)} %fusion.8, f32[4096]{0:T(1024)S(1)} %bitcast.147), kind=kCustom, calls=%fused_computation.18 | custom fusion | flops 4096 | bytes 65536 | tf_op jit(solution)/shard_map/scatter-add | solution.py:93
  164.5 6.2 gather_fusion.4
  170.6 6.2 gather_fusion.5
  176.8 6.2 gather_fusion.7
  183.0 40.6 %gather_fusion.6 = f32[4096]{0:T(1024)} fusion(f32[8193]{0:T(1024)S(1)} %pad_maximum_fusion.4, s32[4096]{0:T(1024)S(1)} %broadcast_clamp_fusion), kind=kCustom, calls=%fused_computation.6 | custom fusion | bytes 49152 | tf_op jit(solution)/shard_map/gather | solution.py:90
  235.7 9.4 %all-to-all-start.1 = ((f32[32,1,128]{2,1,0:T(1,128)}), f32[32,1,128]{2,1,0:T(1,128)S(1)}, u32[]{:S(2)}, u32[]{:S(2)}) async-start(f32[32,1,128]{2,1,0:T(1,128)} %bitcast.22), calls=%async_computation.1 | async-start | bytes 32768 | tf_op jit(solution)/shard_map/all_to_all | solution.py:91
  253.6 26.0 %scatter_fusion.7 = f32[8193]{0:T(1024)S(1)} fusion(f32[8193]{0:T(1024)S(1)} %pad_maximum_fusion.5, s32[4096]{0:T(1024)S(1)} %fusion.8, f32[4096]{0:T(1024)S(1)} %bitcast.148), kind=kCustom, calls=%fused_computation.23 | custom fusion | flops 4096 | bytes 65536 | tf_op jit(solution)/shard_map/scatter-add | solution.py:93
  287.8 101.2 %all-reduce = (f32[]{:T(128)}, f32[]{:T(128)}) all-reduce(f32[]{:T(128)} %get-tuple-element.3, f32[]{:T(128)} %get-tuple-element.2), channel_id=1, replica_groups=mesh['grp'=16,'sub'=32] {'grp','sub'}, use_global_device_ids=true, to_apply=%region_1.0 | all-reduce | flops 2 | bytes 16 | tf_op jit(solution)/shard_map/psum | solution.py:64
  420.5 98.9 %psum.30 = f32[]{:T(128)} all-reduce(f32[]{:T(128)} %get-tuple-element.28), channel_id=1, replica_groups=mesh['grp'=16,'sub'=32] {'grp','sub'}, use_global_device_ids=true, to_apply=%region_15.0 | all-reduce | flops 1 | bytes 8 | tf_op jit(solution)/shard_map/psum | solution.py:64
  526.9 6.2 gather_fusion.9
  533.1 6.2 gather_fusion.11
  539.2 40.6 %gather_fusion.10 = f32[4096]{0:T(1024)} fusion(f32[8193]{0:T(1024)S(1)} %pad_maximum_fusion.2, s32[4096]{0:T(1024)S(1)} %broadcast_clamp_fusion), kind=kCustom, calls=%fused_computation.10 | custom fusion | bytes 49152 | tf_op jit(solution)/shard_map/gather | solution.py:90
  592.0 7.7 all-to-all-start.2
  608.2 26.0 %scatter_fusion.12 = f32[8193]{0:T(1024)S(1)} fusion(f32[8193]{0:T(1024)S(1)} %pad_maximum_fusion.3, s32[4096]{0:T(1024)S(1)} %fusion.8, f32[4096]{0:T(1024)S(1)} %bitcast.149), kind=kCustom, calls=%fused_computation.28 | custom fusion | flops 4096 | bytes 65536 | tf_op jit(solution)/shard_map/scatter-add | solution.py:93
  663.0 40.6 %gather_fusion.14 = f32[4096]{0:T(1024)} fusion(f32[8193]{0:T(1024)S(1)} %pad_maximum_fusion, s32[4096]{0:T(1024)S(1)} %broadcast_clamp_fusion), kind=kCustom, calls=%fused_computation.14 | custom fusion | bytes 49152 | tf_op jit(solution)/shard_map/gather | solution.py:90
  730.3 26.0 %scatter_fusion.17 = f32[8193]{0:T(1024)S(1)} fusion(f32[8193]{0:T(1024)S(1)} %pad_maximum_fusion.1, s32[4096]{0:T(1024)S(1)} %fusion.8, f32[4096]{0:T(1024)S(1)} %bitcast.146), kind=kCustom, calls=%fused_computation.33 | custom fusion | flops 4096 | bytes 65536 | tf_op jit(solution)/shard_map/scatter-add | solution.py:93
  763.8 97.0 %psum.31 = f32[]{:T(128)} all-reduce(f32[]{:T(128)} %multiply_reduce_fusion), channel_id=1, replica_groups=mesh['grp'=16,'sub'=32] {'grp','sub'}, use_global_device_ids=true, to_apply=%region_27.0 | all-reduce | flops 1 | bytes 8 | tf_op jit(solution)/shard_map/psum | solution.py:136
  (178 shorter events, 200.2 us)
Async XLA Ops:
  0.6 31.7 %copy-start = (f32[1,64,64]{2,1,0:T(8,128)S(1)}, f32[1,64,64]{2,1,0:T(8,128)}, u32[]{:S(2)}) copy-start(f32[1,64,64]{2,1,0:T(8,128)} %param.20) | copy-start | bytes 49156
  1.4 31.3 %copy-start.2 = (f32[512,8]{1,0:T(8,128)S(1)}, f32[512,8]{1,0:T(8,128)}, u32[]{:S(2)}) copy-start(f32[512,8]{1,0:T(8,128)} %constant.5.clone) | copy-start | bytes 49156
  3.3 5.4 collective-permute-start
  8.7 5.8 collective-permute-start.1
  14.5 4.3 collective-permute-start.2
  18.8 5.2 collective-permute-start.3
  23.9 8.4 collective-permute-start.4
  104.9 21.8 %all-to-all-start = ((f32[32,1,128]{2,1,0:T(1,128)}), f32[32,1,128]{2,1,0:T(1,128)S(1)}, u32[]{:S(2)}, u32[]{:S(2)}) async-start(f32[32,1,128]{2,1,0:T(1,128)} %bitcast.12), calls=%async_computation | async-start | bytes 32768 | tf_op jit(solution)/shard_map/all_to_all | solution.py:91
  114.2 38.6 %collective-permute-start.5 = (f32[1,512]{1,0:T(1,128)S(1)}, f32[1,512]{1,0:T(1,128)S(1)}, u32[]{:S(2)}, u32[]{:S(2)}) collective-permute-start(f32[1,512]{1,0:T(1,128)S(1)} %bitcast.172), channel_id=1, source_target_pairs={{0,32},{32,64},{64,96},{96,128},{128,160},{160,192},{192,224},{224... | collective-permute-start | bytes 6152 | tf_op jit(solution)/shard_map/ppermute | solution.py:19
  124.8 31.4 %collective-permute-start.6 = (f32[1,512]{1,0:T(1,128)S(1)}, f32[1,512]{1,0:T(1,128)S(1)}, u32[]{:S(2)}, u32[]{:S(2)}) collective-permute-start(f32[1,512]{1,0:T(1,128)S(1)} %bitcast.168), channel_id=1, source_target_pairs={{32,0},{64,32},{96,64},{128,96},{160,128},{192,160},{224,192},{256... | collective-permute-start | bytes 6152 | tf_op jit(solution)/shard_map/ppermute | solution.py:21
  235.7 17.9 %all-to-all-start.1 = ((f32[32,1,128]{2,1,0:T(1,128)}), f32[32,1,128]{2,1,0:T(1,128)S(1)}, u32[]{:S(2)}, u32[]{:S(2)}) async-start(f32[32,1,128]{2,1,0:T(1,128)} %bitcast.22), calls=%async_computation.1 | async-start | bytes 32768 | tf_op jit(solution)/shard_map/all_to_all | solution.py:91
  245.1 34.5 %collective-permute-start.7 = (f32[1,512]{1,0:T(1,128)S(1)}, f32[1,512]{1,0:T(1,128)S(1)}, u32[]{:S(2)}, u32[]{:S(2)}) collective-permute-start(f32[1,512]{1,0:T(1,128)S(1)} %bitcast.173), channel_id=1, source_target_pairs={{0,32},{32,64},{64,96},{96,128},{128,160},{160,192},{192,224},{224... | collective-permute-start | bytes 6152 | tf_op jit(solution)/shard_map/ppermute | solution.py:19
  249.0 34.0 %collective-permute-start.8 = (f32[1,512]{1,0:T(1,128)S(1)}, f32[1,512]{1,0:T(1,128)S(1)}, u32[]{:S(2)}, u32[]{:S(2)}) collective-permute-start(f32[1,512]{1,0:T(1,128)S(1)} %bitcast.169), channel_id=1, source_target_pairs={{32,0},{64,32},{96,64},{128,96},{160,128},{192,160},{224,192},{256... | collective-permute-start | bytes 6152 | tf_op jit(solution)/shard_map/ppermute | solution.py:21
  391.3 4.3 collective-permute-start.9
  395.6 5.8 collective-permute-start.10
  401.3 4.3 collective-permute-start.11
  405.6 5.2 collective-permute-start.12
  410.8 8.2 collective-permute-start.13
  592.0 16.2 %all-to-all-start.2 = ((f32[32,1,128]{2,1,0:T(1,128)}), f32[32,1,128]{2,1,0:T(1,128)S(1)}, u32[]{:S(2)}, u32[]{:S(2)}) async-start(f32[32,1,128]{2,1,0:T(1,128)} %bitcast.33), calls=%async_computation.2 | async-start | bytes 32768 | tf_op jit(solution)/shard_map/all_to_all | solution.py:91
  599.7 34.5 %collective-permute-start.14 = (f32[1,512]{1,0:T(1,128)S(1)}, f32[1,512]{1,0:T(1,128)S(1)}, u32[]{:S(2)}, u32[]{:S(2)}) collective-permute-start(f32[1,512]{1,0:T(1,128)S(1)} %bitcast.174), channel_id=1, source_target_pairs={{0,32},{32,64},{64,96},{96,128},{128,160},{160,192},{192,224},{224... | collective-permute-start | bytes 6152 | tf_op jit(solution)/shard_map/ppermute | solution.py:19
  602.9 34.8 %collective-permute-start.15 = (f32[1,512]{1,0:T(1,128)S(1)}, f32[1,512]{1,0:T(1,128)S(1)}, u32[]{:S(2)}, u32[]{:S(2)}) collective-permute-start(f32[1,512]{1,0:T(1,128)S(1)} %bitcast.170), channel_id=1, source_target_pairs={{32,0},{64,32},{96,64},{128,96},{160,128},{192,160},{224,192},{256... | collective-permute-start | bytes 6152 | tf_op jit(solution)/shard_map/ppermute | solution.py:21
  715.8 14.6 %all-to-all-start.3 = ((f32[32,1,128]{2,1,0:T(1,128)}), f32[32,1,128]{2,1,0:T(1,128)S(1)}, u32[]{:S(2)}, u32[]{:S(2)}) async-start(f32[32,1,128]{2,1,0:T(1,128)} %bitcast.39), calls=%async_computation.3 | async-start | bytes 32768 | tf_op jit(solution)/shard_map/all_to_all | solution.py:91
  721.8 34.6 %collective-permute-start.16 = (f32[1,512]{1,0:T(1,128)S(1)}, f32[1,512]{1,0:T(1,128)S(1)}, u32[]{:S(2)}, u32[]{:S(2)}) collective-permute-start(f32[1,512]{1,0:T(1,128)S(1)} %bitcast.171), channel_id=1, source_target_pairs={{0,32},{32,64},{64,96},{96,128},{128,160},{160,192},{192,224},{224... | collective-permute-start | bytes 6152 | tf_op jit(solution)/shard_map/ppermute | solution.py:19
  725.6 34.1 %collective-permute-start.17 = (f32[1,512]{1,0:T(1,128)S(1)}, f32[1,512]{1,0:T(1,128)S(1)}, u32[]{:S(2)}, u32[]{:S(2)}) collective-permute-start(f32[1,512]{1,0:T(1,128)S(1)} %bitcast.167), channel_id=1, source_target_pairs={{32,0},{64,32},{96,64},{128,96},{160,128},{192,160},{224,192},{256... | collective-permute-start | bytes 6152 | tf_op jit(solution)/shard_map/ppermute | solution.py:21
  (11 other events, 20.9 us)
